TPU v7x, 32 devices: a whole 2x2x4 slice. The times are simulated.
32 devices in a mesh: rep: 2 (over x), node: 8 (over z, y), local: 2 (over core).
Axes of the slice: x: 2, y: 2, z: 4, core: 2. Of those that a mesh axis runs over, the one named last changes fastest.
Arguments:
- tokens: bfloat16 [2048, 7168], P(('rep', 'node', 'local')), parts along dimension 0, may hold values from -6 to 6
- gate_ids: int32 [2048, 4], P(('rep', 'node', 'local')), parts along dimension 0, may hold values from 0 to 7, all different within a row; in each aligned block of 64 rows (0 to 63, 64 to 127, ...) at most 64 rows name the same one
- gate_values: bfloat16 [2048, 4], P(('rep', 'node', 'local')), parts along dimension 0, may hold values from 0.049804688 to 1
- w_gate: bfloat16 [8, 7168, 1024], P('node', None, 'local'), may hold values from -0.0625 to 0.0625
- w_up: bfloat16 [8, 7168, 1024], P('node', None, 'local'), may hold values from -0.0625 to 0.0625
- w_down: bfloat16 [8, 1024, 7168], P('node', 'local'), may hold values from -0.1875 to 0.1875
Outputs:
- mixed: bfloat16 [2048, 7168], P(('rep', 'node', 'local')), parts along dimension 0
There are 2 independent parts, one for each index of `rep`. A program takes and returns all parts, laid end to end along the dimension named above; an argument that names none is the same for every part. Nothing has to cross between parts.
Inputs may be any that keep to these rules, and one draw needn't show every extreme that they name: `gate_ids`: each row names 4 different experts. Within the rows of one device, no expert is named by more than 64 rows, and in every draw some expert is named by exactly 64 rows of some device.
All inputs are finite; a program needn't handle non-finite values.
Results may differ from a plain program's by a relative error of at most 0.0065.
Values may be sent and summed in bfloat16 or wider, within the bound.
A program may use at most 128 MiB of HBM per device.

v0:
```python
import jax
import jax.numpy as jnp
from jax import lax
from jax.sharding import PartitionSpec as P


def per_device(tokens, gate_ids, gate_values, w_gate, w_up, w_down):
    node_count = lax.axis_size("node")
    token_count = tokens.shape[0]
    choose_count = gate_ids.shape[1]
    width = tokens.shape[1]
    capacity = 2 * token_count * choose_count // node_count
    flat_ids = gate_ids.reshape(-1)
    expert_row = jnp.arange(node_count, dtype=jnp.int32)
    onehot = (flat_ids[:, None] == expert_row[None, :]).astype(jnp.int32)
    earlier = jnp.cumsum(onehot, axis=0) - onehot
    within = jnp.sum(earlier * onehot, axis=1)
    slot = (flat_ids * capacity + within).reshape(token_count, choose_count)
    slot_row = jnp.arange(node_count * capacity, dtype=jnp.int32)
    matches = slot[:, :, None] == slot_row[None, None, :]
    select = jnp.any(matches, axis=1).astype(jnp.bfloat16)
    combine_table = jnp.sum(
        jnp.where(matches, gate_values.astype(jnp.float32)[:, :, None], jnp.float32(0.0)), axis=1
    ).astype(jnp.bfloat16)
    outgoing = jnp.einsum("ts,td->sd", select, tokens, preferred_element_type=jnp.float32).astype(
        jnp.bfloat16
    )
    outgoing = outgoing.reshape(node_count, capacity, width)
    gathered = lax.all_gather(
        lax.all_to_all(outgoing, "node", split_axis=0, concat_axis=0, tiled=True),
        "local",
        axis=0,
        tiled=True,
    )
    rows = gathered.reshape(-1, width)
    gate_act = jnp.dot(rows, w_gate[0], preferred_element_type=jnp.float32)
    up_act = jnp.dot(rows, w_up[0], preferred_element_type=jnp.float32)
    hidden = (jax.nn.silu(gate_act) * up_act).astype(jnp.bfloat16)
    partial_value = (
        jnp.dot(hidden, w_down[0], preferred_element_type=jnp.float32)
        .astype(jnp.bfloat16)
        .reshape(gathered.shape)
    )
    partial_value = lax.optimization_barrier(partial_value).astype(jnp.float32)
    own_rows = lax.psum_scatter(
        partial_value.astype(jnp.bfloat16), "local", scatter_dimension=0, tiled=True
    )
    expert_out = lax.all_to_all(own_rows, "node", split_axis=0, concat_axis=0, tiled=True)
    result = jnp.dot(
        combine_table,
        expert_out.reshape(node_count * capacity, width),
        preferred_element_type=jnp.float32,
    )
    return result.astype(jnp.bfloat16)


def solution(mesh):
    return jax.shard_map(
        per_device,
        mesh=mesh,
        in_specs=(
            P(("rep", "node", "local"), None),
            P(("rep", "node", "local"), None),
            P(("rep", "node", "local"), None),
            P("node", None, "local"),
            P("node", None, "local"),
            P("node", "local", None),
        ),
        out_specs=P(("rep", "node", "local"), None),
        check_vma=False,
    )
```

profile of v0, /device:TPU:0, one launch (start us, length us, event | category | flops | bytes accessed | tf_op | source)
XLA Modules:
  0.0 445.9 jit_solution(14984800012365417282)
XLA Ops:
  6.5 0.0 copy-start
  6.5 0.0 all-gather.2.cloned.1.call-start
  6.5 0.9 copy.24
  7.4 0.1 eq.42
  7.5 0.1 eq.38
  7.6 0.6 reduce-window.6
  8.2 0.2 slice_reduce_fusion
  8.5 0.1 fusion.10
  8.6 0.1 reduce_sum.21
  8.7 0.1 copy.26
  8.7 0.7 multiply_add_fusion
  9.4 0.1 fusion.7
  9.6 0.0 copy-done
  9.6 2.1 convolution_convert_fusion.1
  11.7 167.8 %all_to_all.10 = bf16[8,64,7168]{2,1,0:T(8,128)(2,1)} all-to-all(bf16[8,64,7168]{2,1,0:T(8,128)(2,1)S(1)} %bitcast.30), channel_id=1, replica_groups=mesh['rep'=2,'node'=8,'local'=2] {'node'}, dimensions={0} | all-to-all | bytes 14680064 | tf_op jit(solution)/shard_map/all_to_all | solution.py:30
  179.5 0.0 all-gather.2.cloned.1.call-update
  179.5 0.0 reduce-scatter.2.cloned.1.call-start
  179.6 26.1 %all-gather.2.cloned.1.call-done = bf16[16,64,7168]{2,1,0:T(8,128)(2,1)} async-done(((bf16[8,64,7168]{2,1,0:T(8,128)(2,1)}), bf16[16,64,7168]{2,1,0:T(8,128)(2,1)}) %all-gather.2.cloned.1.call-update) | async-done | bytes 14680080 | tf_op jit(solution)/shard_map/all_gather | solution.py:29
  205.7 0.0 copy-start.3
  205.7 0.0 slice-start
  205.7 13.4 %fusion.1 = f32[1024,512]{1,0:T(8,128)S(1)} fusion(bf16[1024,7168]{1,0:T(8,128)(2,1)} %bitcast.32, bf16[1,7168,512]{2,1,0:T(8,128)(2,1)} %param.10), kind=kOutput, calls=%fused_computation.4 | convolution fusion | flops 7516192768 | bytes 24117248 | tf_op jit(solution)/shard_map/dot_general | solution.py:37
  219.1 0.0 copy-done.3
  219.1 0.0 slice-start.1
  219.1 10.3 %multiply_convert_fusion = bf16[1024,512]{1,0:T(8,128)(2,1)S(1)} fusion(f32[1024,512]{1,0:T(8,128)S(1)} %fusion.1, bf16[1024,7168]{1,0:T(8,128)(2,1)S(1)} %bitcast.33, bf16[1,7168,512]{2,1,0:T(8,128)(2,1)} %param.9), kind=kOutput, calls=%fused_computation.8 | convolution fusion | flops 7519338496 | bytes 25165824 | tf_op jit(solution)/shard_map/dot_general | solution.py:36
  229.4 0.0 slice-done
  229.4 0.0 slice-done.1
  229.4 11.1 %convolution_convert_fusion = bf16[1024,7168]{1,0:T(8,128)(2,1)} fusion(bf16[1024,512]{1,0:T(8,128)(2,1)S(1)} %multiply_convert_fusion, bf16[1,512,7168]{2,1,0:T(8,128)(2,1)S(1)} %bitcast.35), kind=kOutput, calls=%fused_computation | convolution fusion | flops 7523532800 | bytes 23068672 | tf_op jit(solution)/shard_map/dot_general | solution.py:40
  240.5 0.0 reduce-scatter.2.cloned.1.call-update
  240.5 0.0 copy-start.2
  240.5 26.1 %reduce-scatter.2.cloned.1.call-done = bf16[8,64,7168]{2,1,0:T(8,128)(2,1)} async-done(((bf16[16,64,7168]{2,1,0:T(8,128)(2,1)}), bf16[8,64,7168]{2,1,0:T(8,128)(2,1)}) %reduce-scatter.2.cloned.1.call-update) | async-done | bytes 7340048 | tf_op jit(solution)/shard_map/reduce_scatter | solution.py:45
  266.7 5.9 %all-to-all-start.1 = ((bf16[8,64,7168]{2,1,0:T(8,128)(2,1)}), bf16[8,64,7168]{2,1,0:T(8,128)(2,1)}, u32[]{:S(2)}, u32[]{:S(2)}) async-start(bf16[8,64,7168]{2,1,0:T(8,128)(2,1)} %reduce-scatter.2.cloned.1.call-done), calls=%async_computation.2 | async-start | bytes 14680064 | tf_op jit(solution)/shard_map/all_to_all | solution.py:48
  272.6 0.0 copy-done.2
  272.6 0.0 copy-start.1
  272.6 0.1 select_reduce_fusion
  272.7 160.8 %all-to-all-done.1 = bf16[8,64,7168]{2,1,0:T(8,128)(2,1)} async-done(((bf16[8,64,7168]{2,1,0:T(8,128)(2,1)}), bf16[8,64,7168]{2,1,0:T(8,128)(2,1)}, u32[]{:S(2)}, u32[]{:S(2)}) %all-to-all-start.1) | async-done | bytes 7340064 | tf_op jit(solution)/shard_map/all_to_all | solution.py:48
  433.6 5.4 %convolution_convert_fusion.2 = bf16[64,7168]{1,0:T(8,128)(2,1)} fusion(bf16[512,7168]{1,0:T(8,128)(2,1)} %bitcast.8, bf16[64,512]{1,0:T(8,128)(2,1)S(1)} %select_reduce_fusion), kind=kOutput, calls=%fused_computation.2 | convolution fusion | flops 470220800 | bytes 8323072 | tf_op jit(solution)/shard_map/dot_general | solution.py:49
  439.0 0.0 copy-done.1
  (5 shorter events, 0.1 us)
Async XLA Ops:
  6.5 3.1 copy-start
  6.5 199.2 %all-gather.2.cloned.1.call-start = ((), (), s32[]{:S(2)}) async-start(), calls=%async_computation.3 | async-start | bytes 22020096 | tf_op jit(solution)/shard_map/all_gather | solution.py:29
  179.5 87.1 %reduce-scatter.2.cloned.1.call-start = ((), (), s32[]{:S(2)}) async-start(), calls=%async_computation.4 | async-start | bytes 22020096 | tf_op jit(solution)/shard_map/reduce_scatter | solution.py:45
  205.7 13.4 %copy-start.3 = (bf16[16,64,7168]{2,1,0:T(8,128)(2,1)S(1)}, bf16[16,64,7168]{2,1,0:T(8,128)(2,1)}, u32[]{:S(2)}) copy-start(bf16[16,64,7168]{2,1,0:T(8,128)(2,1)} %all-gather.2.cloned.1.call-done) | copy-start | bytes 44040196
  205.7 23.7 %slice-start = ((s8[7340032]{0:T(1024)(128)(4,1)}), s8[4194304]{0:T(1024)(128)(4,1)S(1)}, s32[]{:S(2)}) async-start(s8[7340032]{0:T(1024)(128)(4,1)} %bitcast.34), calls=%async_computation.5 | async-start | bytes 8388608
  219.1 10.3 %slice-start.1 = ((s8[7340032]{0:T(1024)(128)(4,1)}), s8[3145728]{0:T(1024)(128)(4,1)S(1)}, s32[]{:S(2)}) async-start(s8[7340032]{0:T(1024)(128)(4,1)} %bitcast.34), calls=%async_computation.6 | async-start | bytes 6291456
  240.5 32.1 %copy-start.2 = (bf16[64,4]{0,1:T(4,128)(2,1)S(1)}, bf16[64,4]{0,1:T(4,128)(2,1)}, u32[]{:S(2)}) copy-start(bf16[64,4]{0,1:T(4,128)(2,1)} %param.8) | copy-start | bytes 1540
  266.7 166.9 %all-to-all-start.1 = ((bf16[8,64,7168]{2,1,0:T(8,128)(2,1)}), bf16[8,64,7168]{2,1,0:T(8,128)(2,1)}, u32[]{:S(2)}, u32[]{:S(2)}) async-start(bf16[8,64,7168]{2,1,0:T(8,128)(2,1)} %reduce-scatter.2.cloned.1.call-done), calls=%async_computation.2 | async-start | bytes 14680064 | tf_op jit(solution)/shard_map/all_to_all | solution.py:48
  272.6 166.4 %copy-start.1 = (bf16[64,7168]{1,0:T(8,128)(2,1)S(1)}, bf16[64,7168]{1,0:T(8,128)(2,1)}, u32[]{:S(2)}) copy-start(bf16[64,7168]{1,0:T(8,128)(2,1)} %param.6) | copy-start | bytes 2752516
Sparse Core Ops, SparseCore 0:
  179.7 26.0 all-gather.1
  240.6 25.9 reduce-scatter.1
where the time goes:
time: 446 us
  waiting for transfers between devices  213 us (48%)
  blocking collectives  168 us (38%)
  matrix products  42.2 us (9%)
  between operations  13.5 us (3%)
  starting transfers between devices  5.94 us (1%)
    all_to_all x1, blocking collectives, per_device(): lax.all_to_all(outgoing, 'node', split_axis=0, concat_axis=0, tiled=True)  168 us
    all_to_all x1, waiting for transfers between devices, per_device(): lax.all_to_all(own_rows, 'node', split_axis=0, concat_axis=0, tiled=True)  161 us
    reduce_scatter x1, waiting for transfers between devices, per_device(): lax.psum_scatter(partial_value.astype(jnp.bfloat16), 'local', scatter_dim...  26.1 us
    all_gather x1, waiting for transfers between devices, per_device(): lax.all_gather(lax.all_to_all(outgoing, 'node', split_axis=0, concat_axis...  26.1 us
    dot_general x1, matrix products, per_device(): up_act = jnp.dot(rows, w_up[0], preferred_element_type=jnp.float32)  13.4 us
    dot_general x1, matrix products, per_device(): jnp.dot(hidden, w_down[0], preferred_element_type=jnp.float32)  11.1 us
    dot_general x1, matrix products, per_device(): gate_act = jnp.dot(rows, w_gate[0], preferred_element_type=jnp.float32)  10.3 us
  transfers between devices with their start and end apart: 3, of which 3 were waited for; matrix products, arithmetic and copies ran while one was open for 0% of the time, Pallas kernels for 0%

commit v1 on v0

--- a/solution.py
+++ b/solution.py
@@ -26,12 +26,11 @@
         jnp.bfloat16
     )
     outgoing = outgoing.reshape(node_count, capacity, width)
-    gathered = lax.all_gather(
-        lax.all_to_all(outgoing, "node", split_axis=0, concat_axis=0, tiled=True),
-        "local",
-        axis=0,
-        tiled=True,
-    )
+    block = lax.all_to_all(outgoing, "node", split_axis=0, concat_axis=0, tiled=True)
+    count = lax.axis_size("local")
+    parts = jnp.stack([block for _ in range(count)])
+    parts = lax.all_to_all(parts, "local", split_axis=0, concat_axis=0)
+    gathered = jnp.concatenate(parts, axis=0)
     rows = gathered.reshape(-1, width)
     gate_act = jnp.dot(rows, w_gate[0], preferred_element_type=jnp.float32)
     up_act = jnp.dot(rows, w_up[0], preferred_element_type=jnp.float32)

time: 446 us -> 432 us (0.969)
  waiting for transfers between devices: 213 us -> 185 us
  blocking collectives: 168 us -> 183 us
    all_gather x1 -> x0, waiting for transfers between devices: 26.1 us -> none  [per_device(): lax.all_gather(lax.all_to_all(outgoing, 'node', split_axis=0, concat_axis...]
    all_to_all x0 -> x1, blocking collectives: none -> 15.8 us  [per_device(): parts = lax.all_to_all(parts, 'local', split_axis=0, concat_axis=0)]
    dot_general x1, matrix products: 13.4 us -> 7.71 us  [per_device(): up_act = jnp.dot(rows, w_up[0], preferred_element_type=jnp.float32)]
  transfers between devices with their start and end apart: 3 -> 2, of which waited for: 3 -> 2; matrix products, arithmetic and copies ran while one was open for 0% -> 0% of each run, Pallas kernels for 0% -> 0%
where the time goes in v1:
time: 432 us
  waiting for transfers between devices  185 us (43%)
  blocking collectives  183 us (42%)
  matrix products  39.4 us (9%)
  between operations  13.5 us (3%)
  starting transfers between devices  5.91 us (1%)
    all_to_all x1, blocking collectives, per_device(): lax.all_to_all(outgoing, 'node', split_axis=0, concat_axis=0, tiled=True)  168 us
    all_to_all x1, waiting for transfers between devices, per_device(): lax.all_to_all(own_rows, 'node', split_axis=0, concat_axis=0, tiled=True)  161 us
    reduce_scatter x1, waiting for transfers between devices, per_device(): lax.psum_scatter(partial_value.astype(jnp.bfloat16), 'local', scatter_dim...  24 us
    all_to_all x1, blocking collectives, per_device(): parts = lax.all_to_all(parts, 'local', split_axis=0, concat_axis=0)  15.8 us
    dot_general x1, matrix products, per_device(): jnp.dot(hidden, w_down[0], preferred_element_type=jnp.float32)  14.1 us
    dot_general x1, matrix products, per_device(): gate_act = jnp.dot(rows, w_gate[0], preferred_element_type=jnp.float32)  10.1 us
  transfers between devices with their start and end apart: 2, of which 2 were waited for; matrix products, arithmetic and copies ran while one was open for 0% of the time, Pallas kernels for 0%

profile of v1, /device:TPU:0, one launch (start us, length us, event | category | flops | bytes accessed | tf_op | source)
XLA Modules:
  0.0 431.6 jit_solution(12388343673521004792)
XLA Ops:
  6.5 0.0 copy-start
  6.5 0.0 reduce-scatter.2.cloned.1.call-start
  6.5 0.9 copy.19
  7.4 0.1 eq.42
  7.5 0.1 eq.38
  7.6 0.6 reduce-window.6
  8.2 0.2 slice_reduce_fusion
  8.5 0.1 fusion.10
  8.6 0.1 reduce_sum.21
  8.7 0.1 copy.21
  8.7 0.7 multiply_add_fusion
  9.4 0.1 fusion.7
  9.6 0.0 copy-done
  9.6 2.1 convolution_convert_fusion.1
  11.7 167.7 %all_to_all.15 = bf16[8,64,7168]{2,1,0:T(8,128)(2,1)S(1)} all-to-all(bf16[8,64,7168]{2,1,0:T(8,128)(2,1)S(1)} %bitcast.31), channel_id=1, replica_groups=mesh['rep'=2,'node'=8,'local'=2] {'node'}, dimensions={0} | all-to-all | bytes 14680064 | tf_op jit(solution)/shard_map/all_to_all | solution.py:29
  179.4 0.0 slice-start
  179.4 1.4 pad_maximum_fusion
  180.8 0.0 slice-start.1
  180.8 15.8 %all_to_all.16 = bf16[2,8,64,7168]{3,2,1,0:T(8,128)(2,1)S(1)} all-to-all(bf16[2,8,64,7168]{3,2,1,0:T(8,128)(2,1)S(1)} %pad_maximum_fusion), channel_id=1, replica_groups=mesh['rep'=2,'node'=8,'local'=2] {'local'}, dimensions={0} | all-to-all | bytes 29360128 | tf_op jit(solution)/shard_map/all_to_all | solution.py:32
  196.6 0.0 slice-done
  196.6 0.0 slice-done.1
  196.6 7.7 %fusion.1 = f32[1024,512]{1,0:T(8,128)S(1)} fusion(bf16[1024,7168]{1,0:T(8,128)(2,1)S(1)} %bitcast.34, bf16[1,7168,512]{2,1,0:T(8,128)(2,1)S(1)} %bitcast.37), kind=kOutput, calls=%fused_computation.5 | convolution fusion | flops 7516192768 | bytes 24117248 | tf_op jit(solution)/shard_map/dot_general | solution.py:36
  204.3 10.1 %multiply_convert_fusion = bf16[1024,512]{1,0:T(8,128)(2,1)S(1)} fusion(f32[1024,512]{1,0:T(8,128)S(1)} %fusion.1, bf16[1024,7168]{1,0:T(8,128)(2,1)S(1)} %bitcast.35, bf16[1,7168,512]{2,1,0:T(8,128)(2,1)} %param.9), kind=kOutput, calls=%fused_computation.9 | convolution fusion | flops 7519338496 | bytes 25165824 | tf_op jit(solution)/shard_map/dot_general | solution.py:35
  214.4 14.1 %convolution_convert_fusion = bf16[1024,7168]{1,0:T(8,128)(2,1)} fusion(bf16[1024,512]{1,0:T(8,128)(2,1)S(1)} %multiply_convert_fusion, bf16[1,512,7168]{2,1,0:T(8,128)(2,1)} %param.11), kind=kOutput, calls=%fused_computation.1 | convolution fusion | flops 7523532800 | bytes 23068672 | tf_op jit(solution)/shard_map/dot_general | solution.py:39
  228.5 0.0 reduce-scatter.2.cloned.1.call-update
  228.5 0.0 copy-start.2
  228.5 24.0 %reduce-scatter.2.cloned.1.call-done = bf16[8,64,7168]{2,1,0:T(8,128)(2,1)} async-done(((bf16[16,64,7168]{2,1,0:T(8,128)(2,1)}), bf16[8,64,7168]{2,1,0:T(8,128)(2,1)}) %reduce-scatter.2.cloned.1.call-update) | async-done | bytes 7340048 | tf_op jit(solution)/shard_map/reduce_scatter | solution.py:44
  252.5 5.9 %all-to-all-start.2 = ((bf16[8,64,7168]{2,1,0:T(8,128)(2,1)}), bf16[8,64,7168]{2,1,0:T(8,128)(2,1)}, u32[]{:S(2)}, u32[]{:S(2)}) async-start(bf16[8,64,7168]{2,1,0:T(8,128)(2,1)} %reduce-scatter.2.cloned.1.call-done), calls=%async_computation.3 | async-start | bytes 14680064 | tf_op jit(solution)/shard_map/all_to_all | solution.py:47
  258.4 0.0 copy-done.2
  258.4 0.0 copy-start.1
  258.4 0.1 select_reduce_fusion
  258.6 160.8 %all-to-all-done.2 = bf16[8,64,7168]{2,1,0:T(8,128)(2,1)} async-done(((bf16[8,64,7168]{2,1,0:T(8,128)(2,1)}), bf16[8,64,7168]{2,1,0:T(8,128)(2,1)}, u32[]{:S(2)}, u32[]{:S(2)}) %all-to-all-start.2) | async-done | bytes 7340064 | tf_op jit(solution)/shard_map/all_to_all | solution.py:47
  419.4 5.4 %convolution_convert_fusion.2 = bf16[64,7168]{1,0:T(8,128)(2,1)} fusion(bf16[512,7168]{1,0:T(8,128)(2,1)} %bitcast.9, bf16[64,512]{1,0:T(8,128)(2,1)S(1)} %select_reduce_fusion), kind=kOutput, calls=%fused_computation.3 | convolution fusion | flops 470220800 | bytes 8323072 | tf_op jit(solution)/shard_map/dot_general | solution.py:48
  424.8 0.0 copy-done.1
  (5 shorter events, 0.1 us)
Async XLA Ops:
  6.5 3.1 copy-start
  6.5 245.9 %reduce-scatter.2.cloned.1.call-start = ((), (), s32[]{:S(2)}) async-start(), calls=%async_computation.4 | async-start | bytes 22020096 | tf_op jit(solution)/shard_map/reduce_scatter | solution.py:44
  179.4 17.2 %slice-start = ((s8[7340032]{0:T(1024)(128)(4,1)}), s8[4194304]{0:T(1024)(128)(4,1)S(1)}, s32[]{:S(2)}) async-start(s8[7340032]{0:T(1024)(128)(4,1)} %bitcast.36), calls=%async_computation.5 | async-start | bytes 8388608
  180.8 15.8 %slice-start.1 = ((s8[7340032]{0:T(1024)(128)(4,1)}), s8[3145728]{0:T(1024)(128)(4,1)S(1)}, s32[]{:S(2)}) async-start(s8[7340032]{0:T(1024)(128)(4,1)} %bitcast.36), calls=%async_computation.6 | async-start | bytes 6291456
  228.5 29.9 %copy-start.2 = (bf16[64,4]{0,1:T(4,128)(2,1)S(1)}, bf16[64,4]{0,1:T(4,128)(2,1)}, u32[]{:S(2)}) copy-start(bf16[64,4]{0,1:T(4,128)(2,1)} %param.8) | copy-start | bytes 1540
  252.5 166.9 %all-to-all-start.2 = ((bf16[8,64,7168]{2,1,0:T(8,128)(2,1)}), bf16[8,64,7168]{2,1,0:T(8,128)(2,1)}, u32[]{:S(2)}, u32[]{:S(2)}) async-start(bf16[8,64,7168]{2,1,0:T(8,128)(2,1)} %reduce-scatter.2.cloned.1.call-done), calls=%async_computation.3 | async-start | bytes 14680064 | tf_op jit(solution)/shard_map/all_to_all | solution.py:47
  258.4 166.4 %copy-start.1 = (bf16[64,7168]{1,0:T(8,128)(2,1)S(1)}, bf16[64,7168]{1,0:T(8,128)(2,1)}, u32[]{:S(2)}) copy-start(bf16[64,7168]{1,0:T(8,128)(2,1)} %param.6) | copy-start | bytes 2752516
Sparse Core Ops, SparseCore 0:
  228.6 23.8 reduce-scatter.1
